TPU v7x, 32 devices: a whole 2x2x4 slice. The times are simulated.
32 devices in a mesh: row: 4 (over z), col: 8 (over y, x, core).
Axes of the slice: x: 2, y: 2, z: 4, core: 2. Of those that a mesh axis runs over, the one named last changes fastest.
Arguments:
- cotangent: float32 [4096, 8192], P('row', 'col'), may hold values from -6 to 6
- whitened: float32 [4096, 8192], P('row', 'col'), may hold values from -0.0625 to 0.0625
- panel_rows: float32 [4, 256, 4096], P(None, None, 'row'), may hold values from -0.375 to 0.375
- diag_inverse: float32 [4, 256, 256], replicated, as said below
Outputs:
- adjoint_rhs: float32 [4096, 8192], P('row', 'col')
- factor_grad: float32 [4, 256, 4096], P(None, 'col', 'row')
Inputs may be any that keep to these rules, and one draw needn't show every extreme that they name: `diag_inverse`: each block is lower triangular with diagonal entries between 0.5 and 1.5.
All inputs are finite; a program needn't handle non-finite values.
Results may differ from a plain program's by a relative error of at most 0.00017.
Values sent between devices are 32-bit elements; how exact they have to be, the bound alone decides.
A program may use at most 128 MiB of HBM per device.

v0:
```python
import jax
import jax.numpy as jnp
from jax import lax
from jax.sharding import PartitionSpec as P


def broadcast(array, axis, root):
    mine = lax.axis_index(axis) == root
    return lax.psum(jnp.where(mine, array, jnp.zeros_like(array)), axis)


def grad_mask(count, natural, within, target):
    inner = jnp.arange(count, dtype=jnp.int32)
    return (natural[None, :] < target) | (natural[None, :] == target) & (
        inner[:, None] >= within[None, :]
    )


def body(cotangent, whitened, panel_rows, diag_inverse):
    hi = lax.Precision.HIGHEST
    n_row = lax.axis_size("row")
    rows_dev = cotangent.shape[0]
    width = diag_inverse.shape[1]
    panel_count = panel_rows.shape[0]
    blocks = rows_dev // width * n_row
    device = lax.axis_index("row")
    local = jnp.arange(rows_dev, dtype=jnp.int32)
    natural = local // width * n_row + device
    within = local % width
    residual = cotangent
    terms = []
    for p in range(panel_count):
        target = blocks - 1 - p
        root = n_row - 1 - p
        own = residual[rows_dev - width :]
        solved = jnp.dot(diag_inverse[p].T, own, precision=hi, preferred_element_type=jnp.float32)
        solved = broadcast(solved, "row", root)
        masked = jnp.where((natural < target)[None, :], panel_rows[p], 0.0)
        update = lax.dot_general(
            masked,
            solved,
            (((0,), (0,)), ((), ())),
            precision=hi,
            preferred_element_type=jnp.float32,
        )
        residual = residual - update
        tail = jnp.where(device == root, solved, residual[rows_dev - width :])
        residual = jnp.concatenate([residual[: rows_dev - width], tail], 0)
        partial_term = lax.dot_general(
            solved,
            whitened,
            (((1,), (1,)), ((), ())),
            precision=hi,
            preferred_element_type=jnp.float32,
        )
        terms.append(jnp.where(grad_mask(width, natural, within, target), -partial_term, 0.0))
    factor_grad = lax.psum_scatter(jnp.stack(terms), "col", scatter_dimension=1, tiled=True)
    return (residual, factor_grad)


def solution(mesh):
    return jax.shard_map(
        body,
        mesh=mesh,
        in_specs=(P("row", "col"), P("row", "col"), P(None, None, "row"), P()),
        out_specs=(P("row", "col"), P(None, "col", "row")),
        check_vma=False,
    )
```

profile of v0, /device:TPU:0, one launch (start us, length us, event | category | flops | bytes accessed | tf_op | source)
XLA Modules:
  0.0 321.2 jit_solution(1200197251109899264)
XLA Ops:
  7.2 0.0 all-reduce.5.cloned.1.call-start
  7.2 3.3 %convolution_select_fusion.3 = f32[256,1024]{1,0:T(8,128)} fusion(f32[1024,1024]{1,0:T(8,128)} %param.4, pred[]{:T(512)S(6)} %eq.50, f32[4,256,256]{2,1,0:T(8,128)} %param.7), kind=kOutput, calls=%fused_computation.12 | convolution fusion | flops 805568512 | bytes 2359297 | tf_op jit(solution)/shard_map/dot_general | solution.py:36
  10.5 0.0 all-reduce.5.cloned.1.call-update
  10.6 0.0 all-reduce.7.cloned.1.call-start
  10.6 54.9 %all-reduce.5.cloned.1.call-done = f32[256,1024]{1,0:T(8,128)} async-done(((f32[256,1024]{1,0:T(8,128)}), f32[256,1024]{1,0:T(8,128)}) %all-reduce.5.cloned.1.call-update) | async-done | bytes 1048592 | tf_op jit(solution)/shard_map/psum | solution.py:9
  65.6 0.0 copy-start.4
  65.6 6.7 %convolution_subtract_fusion = f32[1024,1024]{1,0:T(8,128)S(1)} fusion(f32[1024,1024]{1,0:T(8,128)} %param.4, f32[256,1024]{1,0:T(8,128)} %all-reduce.5.cloned.1.call-done, f32[4,256,1024]{2,1,0:T(8,128)} %param.6, pred[1024]{0:T(1024)(128)(4,1)S(1)} %fusion.56), kind=kOutput, calls=%fused_computation.5 | convolution fusion | flops 3222536192 | bytes 10486784 | tf_op jit(solution)/shard_map/dot_general | solution.py:39
  72.3 0.0 copy-start.3
  72.3 2.0 copy-done.3
  74.3 0.0 copy-done.4
  74.3 0.1 slice_select_fusion.3
  74.4 0.0 copy-start.12
  74.4 1.0 copy-done.12
  75.4 3.0 fusion.2
  78.5 0.0 slice-start.2
  78.5 0.0 all-reduce.7.cloned.1.call-update
  78.5 0.0 all-reduce.9.cloned.1.call-start
  78.6 51.2 %all-reduce.7.cloned.1.call-done = f32[256,1024]{1,0:T(8,128)} async-done(((f32[256,1024]{1,0:T(8,128)}), f32[256,1024]{1,0:T(8,128)}) %all-reduce.7.cloned.1.call-update) | async-done | bytes 1048592 | tf_op jit(solution)/shard_map/psum | solution.py:9
  129.8 0.0 slice-done.2
  129.8 0.0 copy-start.6
  129.8 5.8 %maximum_subtract_fusion = f32[1024,1024]{1,0:T(8,128)S(1)} fusion(f32[256,1024]{1,0:T(8,128)} %copy-done.12, f32[768,1024]{1,0:T(8,128)S(1)} %slice-done.2, f32[256,1024]{1,0:T(8,128)} %all-reduce.7.cloned.1.call-done, f32[4,256,1024]{2,1,0:T(8,128)} %param.6, pred[1024]{0:T(1024)(128)(4,1)S(1)} %fusion.55), kind=kOutput, calls=%fused_computation | convolution fusion | flops 3223584768 | bytes 10486784 | tf_op jit(solution)/shard_map/dot_general | solution.py:39
  135.6 0.0 copy-start.2
  135.6 2.0 copy-done.2
  137.6 0.0 copy-done.6
  137.6 0.1 slice_select_fusion.2
  137.7 0.0 copy-start.11
  137.8 1.0 copy-done.11
  138.7 3.1 fusion.1
  141.8 0.0 all-reduce.9.cloned.1.call-update
  141.8 0.2 all-reduce.11.cloned.1.call-start
  142.1 51.0 %all-reduce.9.cloned.1.call-done = f32[256,1024]{1,0:T(8,128)} async-done(((f32[256,1024]{1,0:T(8,128)}), f32[256,1024]{1,0:T(8,128)}) %all-reduce.9.cloned.1.call-update) | async-done | bytes 1048592 | tf_op jit(solution)/shard_map/psum | solution.py:9
  193.1 0.0 slice-done.1
  193.1 5.8 %maximum_subtract_fusion.1 = f32[1024,1024]{1,0:T(8,128)S(1)} fusion(f32[256,1024]{1,0:T(8,128)} %copy-done.11, f32[768,1024]{1,0:T(8,128)S(1)} %slice-done.1, f32[256,1024]{1,0:T(8,128)} %all-reduce.9.cloned.1.call-done, f32[4,256,1024]{2,1,0:T(8,128)} %param.6, pred[1024]{0:T(1024)(128)(4,1)S(1)} %fusion.54), kind=kOutput, calls=%fused_computation.1 | convolution fusion | flops 3223584768 | bytes 10486784 | tf_op jit(solution)/shard_map/dot_general | solution.py:39
  198.9 0.0 copy-start.1
  198.9 2.0 copy-done.1
  200.9 0.0 copy-done.9
  200.9 0.1 slice_select_fusion.1
  201.1 3.1 fusion
  204.2 0.0 all-reduce.11.cloned.1.call-update
  204.2 0.0 reduce-scatter.2.cloned.1.call-start
  204.3 0.0 copy-start
  204.3 0.0 copy-done.5
  204.3 7.1 %fusion.10 = f32[1,256,1024]{2,1,0:T(8,128)} fusion(f32[256,1024]{1,0:T(8,128)S(1)} %copy-done.5, f32[1024,1024]{1,0:T(8,128)} %param.5, s32[1024]{0:T(1024)S(1)} %fusion.40, pred[1024]{0:T(1024)(128)(4,1)S(1)} %get-tuple-element.5, pred[1024]{0:T(1024)(128)(4,1)S(1)} %fusion.56), kind=kOutput, calls=%fused_computation.24 | convolution fusion | flops 3222536192 | bytes 6297600 | tf_op jit(solution)/shard_map/dot_general | solution.py:49
  211.4 0.0 copy-done.7
  211.4 0.0 copy-done
  211.4 4.8 %fusion.8 = f32[1,256,1024]{2,1,0:T(8,128)} fusion(f32[256,1024]{1,0:T(8,128)S(1)} %copy-done.7, f32[1024,1024]{1,0:T(8,128)S(1)} %copy-done, s32[1024]{0:T(1024)S(1)} %fusion.40, pred[1024]{0:T(1024)(128)(4,1)S(1)} %get-tuple-element.4, pred[1024]{0:T(1024)(128)(4,1)S(1)} %fusion.55), kind=kOutput, calls=%fused_computation.21 | convolution fusion | flops 3222536192 | bytes 6297600 | tf_op jit(solution)/shard_map/dot_general | solution.py:49
  216.1 0.0 copy-done.10
  216.1 4.8 %fusion.6 = f32[1,256,1024]{2,1,0:T(8,128)} fusion(f32[256,1024]{1,0:T(8,128)S(1)} %copy-done.10, f32[1024,1024]{1,0:T(8,128)S(1)} %copy-done, s32[1024]{0:T(1024)S(1)} %fusion.40, pred[1024]{0:T(1024)(128)(4,1)S(1)} %get-tuple-element.3, pred[1024]{0:T(1024)(128)(4,1)S(1)} %fusion.54), kind=kOutput, calls=%fused_computation.18 | convolution fusion | flops 3222536192 | bytes 6297600 | tf_op jit(solution)/shard_map/dot_general | solution.py:49
  220.9 34.6 %all-reduce.11.cloned.1.call-done = f32[256,1024]{1,0:T(8,128)} async-done(((f32[256,1024]{1,0:T(8,128)}), f32[256,1024]{1,0:T(8,128)}) %all-reduce.11.cloned.1.call-update) | async-done | bytes 1048592 | tf_op jit(solution)/shard_map/psum | solution.py:9
  255.5 6.2 %fusion.4 = f32[1,256,1024]{2,1,0:T(8,128)S(1)} fusion(f32[256,1024]{1,0:T(8,128)} %all-reduce.11.cloned.1.call-done, f32[1024,1024]{1,0:T(8,128)} %param.5, s32[1024]{0:T(1024)S(1)} %fusion.40, pred[1024]{0:T(1024)(128)(4,1)S(1)} %get-tuple-element.2, pred[1024]{0:T(1024)(128)(4,1)S(1)} %fusion.53), kind=kOutput, calls=%fused_computation.15 | convolution fusion | flops 3222536192 | bytes 6297600 | tf_op jit(solution)/shard_map/dot_general | solution.py:49
  261.7 0.0 copy-done.13
  261.8 0.0 copy-done.14
  261.8 0.0 copy-done.15
  261.8 2.3 pad_maximum_fusion.1
  264.0 0.0 reduce-scatter.2.cloned.1.call-update
  264.1 0.0 slice-start
  264.1 0.0 copy-start.8
  264.1 1.9 slice-done
  266.0 0.3 copy-done.8
  266.2 5.0 %maximum_subtract_fusion.2 = f32[1024,1024]{1,0:T(8,128)S(1)} fusion(f32[256,1024]{1,0:T(8,128)S(1)} %slice_select_fusion.1, f32[768,1024]{1,0:T(8,128)S(1)} %slice-done, f32[256,1024]{1,0:T(8,128)S(1)} %copy-done.8, f32[4,256,1024]{2,1,0:T(8,128)} %param.6, pred[1024]{0:T(1024)(128)(4,1)S(1)} %fusion.53), kind=kOutput, calls=%fused_computation.2 | convolution fusion | flops 3223584768 | bytes 10486784 | tf_op jit(solution)/shard_map/dot_general | solution.py:39
  271.3 0.4 slice.74
  271.7 0.2 slice_select_fusion
  271.8 2.3 pad_maximum_fusion
  274.2 40.5 %reduce-scatter.2.cloned.1.call-done = f32[4,32,1024]{2,1,0:T(8,128)} async-done(((f32[4,256,1024]{2,1,0:T(8,128)}), f32[4,32,1024]{2,1,0:T(8,128)}) %reduce-scatter.2.cloned.1.call-update) | async-done | bytes 524304 | tf_op jit(solution)/shard_map/reduce_scatter | solution.py:57
  (15 shorter events, 0.1 us)
Async XLA Ops:
  7.2 58.4 %all-reduce.5.cloned.1.call-start = ((), (), s32[]{:S(2)}) async-start(), calls=%async_computation.1 | async-start | bytes 2097152 | tf_op jit(solution)/shard_map/psum | solution.py:9
  10.6 119.2 %all-reduce.7.cloned.1.call-start = ((), (), s32[]{:S(2)}) async-start(), calls=%async_computation.2 | async-start | bytes 2097152 | tf_op jit(solution)/shard_map/psum | solution.py:9
  65.6 8.7 %copy-start.4 = (f32[256,1024]{1,0:T(8,128)S(1)}, f32[256,1024]{1,0:T(8,128)}, u32[]{:S(2)}) copy-start(f32[256,1024]{1,0:T(8,128)} %all-reduce.5.cloned.1.call-done) | copy-start | bytes 3145732
  72.3 2.0 copy-start.3
  74.4 1.0 copy-start.12
  78.5 51.3 %slice-start.2 = ((f32[1024,1024]{1,0:T(8,128)}), f32[768,1024]{1,0:T(8,128)S(1)}, s32[]{:S(2)}) async-start(f32[1024,1024]{1,0:T(8,128)} %copy-done.3), calls=%async_computation.8 | async-start | bytes 6291456 | tf_op jit(solution)/shard_map/slice | solution.py:48
  78.5 114.6 %all-reduce.9.cloned.1.call-start = ((), (), s32[]{:S(2)}) async-start(), calls=%async_computation.3 | async-start | bytes 2097152 | tf_op jit(solution)/shard_map/psum | solution.py:9
  129.8 7.8 %copy-start.6 = (f32[256,1024]{1,0:T(8,128)S(1)}, f32[256,1024]{1,0:T(8,128)}, u32[]{:S(2)}) copy-start(f32[256,1024]{1,0:T(8,128)} %all-reduce.7.cloned.1.call-done) | copy-start | bytes 3145732
  135.6 2.0 copy-start.2
  137.7 1.0 copy-start.11
  141.8 51.3 %slice-start.1 = ((f32[1024,1024]{1,0:T(8,128)}), f32[768,1024]{1,0:T(8,128)S(1)}, s32[]{:S(2)}) async-start(f32[1024,1024]{1,0:T(8,128)} %copy-done.2), calls=%async_computation.7 | async-start | bytes 6291456 | tf_op jit(solution)/shard_map/slice | solution.py:48
  141.8 113.7 %all-reduce.11.cloned.1.call-start = ((), (), s32[]{:S(2)}) async-start(), calls=%async_computation.4 | async-start | bytes 2097152 | tf_op jit(solution)/shard_map/psum | solution.py:9
  193.1 7.8 %copy-start.9 = (f32[256,1024]{1,0:T(8,128)S(1)}, f32[256,1024]{1,0:T(8,128)}, u32[]{:S(2)}) copy-start(f32[256,1024]{1,0:T(8,128)} %all-reduce.9.cloned.1.call-done) | copy-start | bytes 3145732
  198.9 2.0 copy-start.1
  200.9 3.4 %copy-start.5 = (f32[256,1024]{1,0:T(8,128)S(1)}, f32[256,1024]{1,0:T(8,128)}, u32[]{:S(2)}) copy-start(f32[256,1024]{1,0:T(8,128)} %all-reduce.5.cloned.1.call-done) | copy-start | bytes 3145732
  204.2 7.2 %copy-start.7 = (f32[256,1024]{1,0:T(8,128)S(1)}, f32[256,1024]{1,0:T(8,128)}, u32[]{:S(2)}) copy-start(f32[256,1024]{1,0:T(8,128)} %all-reduce.7.cloned.1.call-done) | copy-start | bytes 3145732
  204.2 110.4 %reduce-scatter.2.cloned.1.call-start = ((), (), s32[]{:S(2)}) async-start(), calls=%async_computation.5 | async-start | bytes 4718592 | tf_op jit(solution)/shard_map/reduce_scatter | solution.py:57
  204.3 7.1 %copy-start = (f32[1024,1024]{1,0:T(8,128)S(1)}, f32[1024,1024]{1,0:T(8,128)}, u32[]{:S(2)}) copy-start(f32[1024,1024]{1,0:T(8,128)} %param.5) | copy-start | bytes 12582916
  211.4 4.8 %copy-start.10 = (f32[256,1024]{1,0:T(8,128)S(1)}, f32[256,1024]{1,0:T(8,128)}, u32[]{:S(2)}) copy-start(f32[256,1024]{1,0:T(8,128)} %all-reduce.9.cloned.1.call-done) | copy-start | bytes 3145732
  220.9 40.9 %copy-start.13 = (f32[1,256,1024]{2,1,0:T(8,128)S(1)}, f32[1,256,1024]{2,1,0:T(8,128)}, u32[]{:S(2)}) copy-start(f32[1,256,1024]{2,1,0:T(8,128)} %fusion.10) | copy-start | bytes 3145732
  220.9 40.9 %copy-start.14 = (f32[1,256,1024]{2,1,0:T(8,128)S(1)}, f32[1,256,1024]{2,1,0:T(8,128)}, u32[]{:S(2)}) copy-start(f32[1,256,1024]{2,1,0:T(8,128)} %fusion.8) | copy-start | bytes 3145732
  255.5 6.3 %copy-start.15 = (f32[1,256,1024]{2,1,0:T(8,128)S(1)}, f32[1,256,1024]{2,1,0:T(8,128)}, u32[]{:S(2)}) copy-start(f32[1,256,1024]{2,1,0:T(8,128)} %fusion.6) | copy-start | bytes 3145732
  264.1 1.9 slice-start
  264.1 2.2 copy-start.8
Sparse Core Ops, SparseCore 0:
  10.9 54.6 all-reduce.4
  78.6 51.1 all-reduce.6
  141.9 51.1 all-reduce.8
  204.3 51.1 all-reduce.10
  264.2 50.3 reduce-scatter.1
where the time goes:
time: 321 us
  waiting for transfers between devices  232 us (72%)
  matrix products  58.6 us (18%)
  between operations  14 us (4%)
  local copies, waits for them, and re-layouts  10.6 us (3%)
  other arithmetic  5.24 us (2%)
    psum x4, waiting for transfers between devices, broadcast(): return lax.psum(jnp.where(mine, array, jnp.zeros_like(array)), axis)  192 us
    reduce_scatter x1, waiting for transfers between devices, body(): lax.psum_scatter(jnp.stack(terms), 'col', scatter_dimension=1, tiled=True)  40.5 us
    dot_general x4, matrix products, body(): lax.dot_general(masked, solved, (((0,), (0,)), ((), ())), precision=hi, p...  23.3 us
    dot_general x4, matrix products, body(): lax.dot_general(solved, whitened, (((1,), (1,)), ((), ())), precision=hi,...  22.8 us
    dot_general x4, matrix products, body(): jnp.dot(diag_inverse[p].T, own, precision=hi, preferred_element_type=jnp....  12.5 us
    unnamed x32, local copies, waits for them, and re-layouts  8.3 us
  transfers between devices with their start and end apart: 5, of which 5 were waited for; matrix products, arithmetic and copies ran while one was open for 8% of the time, Pallas kernels for 0%

commit v1 on v0

--- a/solution.py
+++ b/solution.py
@@ -6,7 +6,7 @@
 
 def broadcast(array, axis, root):
     mine = lax.axis_index(axis) == root
-    return lax.psum(jnp.where(mine, array, jnp.zeros_like(array)), axis)
+    return jnp.sum(lax.all_gather(jnp.where(mine, array, jnp.zeros_like(array)), axis), axis=0)
 
 
 def grad_mask(count, natural, within, target):

time: 321 us -> 494 us (1.54); the launches traced: 321 us -> 488 us
  waiting for transfers between devices: 232 us -> 333 us
  local copies, waits for them, and re-layouts: 10.6 us -> 35.3 us
  matrix products: 58.6 us -> 81.3 us
  other arithmetic: 5.24 us -> 24.4 us
    all_gather x0 -> x4, waiting for transfers between devices: none -> 299 us  [broadcast(): lax.all_gather(jnp.where(mine, array, jnp.zeros_like(array)), axis)]
    psum x4 -> x0, waiting for transfers between devices: 192 us -> none  [broadcast(): return lax.psum(jnp.where(mine, array, jnp.zeros_like(array)), axis)]
    reduce_sum x0 -> x4, other arithmetic: none -> 19 us  [broadcast(): jnp.sum(lax.all_gather(jnp.where(mine, array, jnp.zeros_like(array)), axi...]
    all_gather x0 -> x3, local copies, waits for them, and re-layouts: none -> 17.4 us  [broadcast(): lax.all_gather(jnp.where(mine, array, jnp.zeros_like(array)), axis)]
    dot_general x4, matrix products: 23.3 us -> 34.7 us  [body(): lax.dot_general(masked, solved, (((0,), (0,)), ((), ())), precision=hi, p...]
    dot_general x4, matrix products: 22.8 us -> 32 us  [body(): lax.dot_general(solved, whitened, (((1,), (1,)), ((), ())), precision=hi,...]
    reduce_sum x0 -> x3, local copies, waits for them, and re-layouts: none -> 7.85 us  [broadcast(): jnp.sum(lax.all_gather(jnp.where(mine, array, jnp.zeros_like(array)), axi...]
    reduce_scatter x1, waiting for transfers between devices: 40.5 us -> 34 us  [body(): lax.psum_scatter(jnp.stack(terms), 'col', scatter_dimension=1, tiled=True)]
where the time goes in v1:
time: 494 us; the launch traced here: 488 us
  waiting for transfers between devices  333 us (67%)
  matrix products  81.3 us (16%)
  local copies, waits for them, and re-layouts  35.3 us (7%)
  other arithmetic  24.4 us (5%)
  between operations  14.4 us (3%)
    all_gather x4, waiting for transfers between devices, broadcast(): lax.all_gather(jnp.where(mine, array, jnp.zeros_like(array)), axis)  299 us
    dot_general x4, matrix products, body(): lax.dot_general(masked, solved, (((0,), (0,)), ((), ())), precision=hi, p...  34.7 us
    reduce_scatter x1, waiting for transfers between devices, body(): lax.psum_scatter(jnp.stack(terms), 'col', scatter_dimension=1, tiled=True)  34 us
    dot_general x4, matrix products, body(): lax.dot_general(solved, whitened, (((1,), (1,)), ((), ())), precision=hi,...  32 us
    reduce_sum x4, other arithmetic, broadcast(): jnp.sum(lax.all_gather(jnp.where(mine, array, jnp.zeros_like(array)), axi...  19 us
    all_gather x3, local copies, waits for them, and re-layouts, broadcast(): lax.all_gather(jnp.where(mine, array, jnp.zeros_like(array)), axis)  17.4 us
    dot_general x4, matrix products, body(): jnp.dot(diag_inverse[p].T, own, precision=hi, preferred_element_type=jnp....  14.5 us
  transfers between devices with their start and end apart: 5, of which 5 were waited for; matrix products, arithmetic and copies ran while one was open for 8% of the time, Pallas kernels for 0%

profile of v1, /device:TPU:0, one launch (start us, length us, event | category | flops | bytes accessed | tf_op | source)
XLA Modules:
  0.0 488.4 jit_solution(13795338663058234936)
XLA Ops:
  7.2 0.0 all-gather.9.cloned.1.call-start
  7.2 3.3 convolution_select_fusion.3
  10.5 0.0 all-gather.9.cloned.1.call-update
  10.6 0.0 all-gather.11.cloned.1.call-start
  10.6 83.5 %all-gather.9.cloned.1.call-done = f32[1024,1024]{1,0:T(8,128)} async-done(((f32[256,1024]{1,0:T(8,128)}), f32[1024,1024]{1,0:T(8,128)}) %all-gather.9.cloned.1.call-update) | async-done | bytes 4194320 | tf_op jit(solution)/shard_map/all_gather | solution.py:9
  94.2 2.7 reduce_sum.36
  96.9 0.0 copy-start.4
  96.9 7.6 %convolution_subtract_fusion = f32[1024,1024]{1,0:T(8,128)S(1)} fusion(f32[1024,1024]{1,0:T(8,128)} %param.4, f32[256,1024]{1,0:T(8,128)S(1)} %reduce_sum.36, f32[4,256,1024]{2,1,0:T(8,128)} %param.6, pred[1024]{0:T(1024)(128)(4,1)S(1)} %fusion.56), kind=kOutput, calls=%fused_computation.5 | convolution fusion | flops 3222536192 | bytes 10486784 | tf_op jit(solution)/shard_map/dot_general | solution.py:39
  104.6 1.9 copy-done.3
  106.5 0.2 slice_select_fusion.3
  106.7 1.0 copy-done.11
  107.6 3.7 fusion.2
  111.4 0.0 all-gather.11.cloned.1.call-update
  111.4 0.0 all-gather.13.cloned.1.call-start
  111.5 79.3 %all-gather.11.cloned.1.call-done = f32[1024,1024]{0,1:T(8,128)} async-done(((f32[256,1024]{0,1:T(8,128)}), f32[1024,1024]{0,1:T(8,128)}) %all-gather.11.cloned.1.call-update) | async-done | bytes 4194320 | tf_op jit(solution)/shard_map/all_gather | solution.py:9
  190.8 5.8 %reshape.63 = f32[4,256,1024]{1,0,2:T(4,128)} reshape(f32[1024,1024]{0,1:T(8,128)} %all-gather.11.cloned.1.call-done) | data formatting | bytes 8388608 | tf_op jit(solution)/shard_map/all_gather | solution.py:9
  196.5 0.0 slice-start.2
  196.6 5.8 %reduce_sum.37 = f32[256,1024]{0,1:T(8,128)} reduce(f32[4,256,1024]{1,0,2:T(4,128)} %reshape.63, f32[]{:T(128)} %constant.74.clone.1), dimensions={0}, to_apply=%region_1.2 | reduce | flops 786432 | bytes 5242884 | tf_op jit(solution)/shard_map/reduce_sum | solution.py:9
  202.4 2.5 copy.6
  204.9 0.0 slice-done.2
  204.9 8.9 %maximum_subtract_fusion = f32[1024,1024]{1,0:T(8,128)S(1)} fusion(f32[256,1024]{1,0:T(8,128)} %copy-done.11, f32[768,1024]{1,0:T(8,128)S(1)} %slice-done.2, f32[256,1024]{0,1:T(8,128)} %reduce_sum.37, f32[4,256,1024]{2,1,0:T(8,128)} %param.6, pred[1024]{0:T(1024)(128)(4,1)S(1)} %fusion.55), kind=kOutput, calls=%fused_computation | convolution fusion | flops 3223584768 | bytes 10486784 | tf_op jit(solution)/shard_map/dot_general | solution.py:39
  213.9 0.0 copy-start.2
  213.9 1.9 copy-done.2
  215.8 0.0 copy-done.13
  215.8 0.1 slice_select_fusion.2
  216.0 0.0 copy-start.10
  216.0 1.0 copy-done.10
  216.9 3.7 fusion.1
  220.7 0.0 all-gather.13.cloned.1.call-update
  220.7 0.0 all-gather.15.cloned.1.call-start
  220.8 79.3 %all-gather.13.cloned.1.call-done = f32[1024,1024]{0,1:T(8,128)} async-done(((f32[256,1024]{0,1:T(8,128)}), f32[1024,1024]{0,1:T(8,128)}) %all-gather.13.cloned.1.call-update) | async-done | bytes 4194320 | tf_op jit(solution)/shard_map/all_gather | solution.py:9
  300.1 6.0 %reshape.64 = f32[4,256,1024]{1,0,2:T(4,128)} reshape(f32[1024,1024]{0,1:T(8,128)} %all-gather.13.cloned.1.call-done) | data formatting | bytes 8388608 | tf_op jit(solution)/shard_map/all_gather | solution.py:9
  306.1 0.0 slice-start.1
  306.1 5.8 %reduce_sum.38 = f32[256,1024]{0,1:T(8,128)} reduce(f32[4,256,1024]{1,0,2:T(4,128)} %reshape.64, f32[]{:T(128)} %constant.74.clone.1), dimensions={0}, to_apply=%region_2.3 | reduce | flops 786432 | bytes 5242884 | tf_op jit(solution)/shard_map/reduce_sum | solution.py:9
  311.9 2.5 copy.7
  314.5 8.9 %maximum_subtract_fusion.1 = f32[1024,1024]{1,0:T(8,128)S(1)} fusion(f32[256,1024]{1,0:T(8,128)} %copy-done.10, f32[768,1024]{1,0:T(8,128)S(1)} %slice-done.1, f32[256,1024]{0,1:T(8,128)} %reduce_sum.38, f32[4,256,1024]{2,1,0:T(8,128)} %param.6, pred[1024]{0:T(1024)(128)(4,1)S(1)} %fusion.54), kind=kOutput, calls=%fused_computation.1 | convolution fusion | flops 3223584768 | bytes 10486784 | tf_op jit(solution)/shard_map/dot_general | solution.py:39
  323.4 1.9 copy-done.1
  325.4 0.1 slice_select_fusion.1
  325.5 0.0 copy-start.9
  325.5 1.0 copy-done.9
  326.5 3.7 fusion
  330.2 0.0 all-gather.15.cloned.1.call-update
  330.3 0.0 reduce-scatter.2.cloned.1.call-start
  330.3 0.0 copy-start
  330.4 6.2 %fusion.10 = f32[1,256,1024]{2,1,0:T(8,128)S(1)} fusion(f32[256,1024]{1,0:T(8,128)S(1)} %copy-done.5, f32[1024,1024]{1,0:T(8,128)} %param.5, s32[1024]{0:T(1024)S(1)} %fusion.40, pred[1024]{0:T(1024)(128)(4,1)S(1)} %get-tuple-element.5, pred[1024]{0:T(1024)(128)(4,1)S(1)} %fusion.56), kind=kOutput, calls=%fused_computation.24 | convolution fusion | flops 3222536192 | bytes 6297600 | tf_op jit(solution)/shard_map/dot_general | solution.py:49
  336.6 8.0 %fusion.8 = f32[1,256,1024]{2,1,0:T(8,128)} fusion(f32[256,1024]{0,1:T(8,128)S(1)} %copy-done.6, f32[1024,1024]{1,0:T(8,128)S(1)} %copy-done, s32[1024]{0:T(1024)S(1)} %fusion.40, pred[1024]{0:T(1024)(128)(4,1)S(1)} %get-tuple-element.4, pred[1024]{0:T(1024)(128)(4,1)S(1)} %fusion.55), kind=kOutput, calls=%fused_computation.21 | convolution fusion | flops 3222536192 | bytes 6297600 | tf_op jit(solution)/shard_map/dot_general | solution.py:49
  344.7 8.3 %fusion.6 = f32[1,256,1024]{2,1,0:T(8,128)} fusion(f32[256,1024]{0,1:T(8,128)S(1)} %copy-done.7, f32[1024,1024]{1,0:T(8,128)S(1)} %copy-done, s32[1024]{0:T(1024)S(1)} %fusion.40, pred[1024]{0:T(1024)(128)(4,1)S(1)} %get-tuple-element.3, pred[1024]{0:T(1024)(128)(4,1)S(1)} %fusion.54), kind=kOutput, calls=%fused_computation.18 | convolution fusion | flops 3222536192 | bytes 6297600 | tf_op jit(solution)/shard_map/dot_general | solution.py:49
  353.0 56.7 %all-gather.15.cloned.1.call-done = f32[1024,1024]{0,1:T(8,128)} async-done(((f32[256,1024]{0,1:T(8,128)}), f32[1024,1024]{0,1:T(8,128)}) %all-gather.15.cloned.1.call-update) | async-done | bytes 4194320 | tf_op jit(solution)/shard_map/all_gather | solution.py:9
  409.6 5.6 %reshape.65 = f32[4,256,1024]{1,0,2:T(4,128)} reshape(f32[1024,1024]{0,1:T(8,128)} %all-gather.15.cloned.1.call-done) | data formatting | bytes 8388608 | tf_op jit(solution)/shard_map/all_gather | solution.py:9
  415.3 4.7 reduce_sum.39
  419.9 0.0 copy-start.8
  420.0 9.5 %fusion.4 = f32[1,256,1024]{2,1,0:T(8,128)S(1)} fusion(f32[256,1024]{0,1:T(8,128)S(1)} %reduce_sum.39, f32[1024,1024]{1,0:T(8,128)} %param.5, s32[1024]{0:T(1024)S(1)} %fusion.40, pred[1024]{0:T(1024)(128)(4,1)S(1)} %get-tuple-element.2, pred[1024]{0:T(1024)(128)(4,1)S(1)} %fusion.53), kind=kOutput, calls=%fused_computation.15 | convolution fusion | flops 3222536192 | bytes 6297600 | tf_op jit(solution)/shard_map/dot_general | solution.py:49
  429.5 2.3 pad_maximum_fusion.1
  431.8 0.0 reduce-scatter.2.cloned.1.call-update
  431.8 0.0 slice-start
  431.8 2.8 copy.8
  434.6 0.0 slice-done
  434.6 9.2 %maximum_subtract_fusion.2 = f32[1024,1024]{1,0:T(8,128)S(1)} fusion(f32[256,1024]{1,0:T(8,128)} %copy-done.9, f32[768,1024]{1,0:T(8,128)S(1)} %slice-done, f32[256,1024]{0,1:T(8,128)} %copy-done.8, f32[4,256,1024]{2,1,0:T(8,128)} %param.6, pred[1024]{0:T(1024)(128)(4,1)S(1)} %fusion.53), kind=kOutput, calls=%fused_computation.2 | convolution fusion | flops 3223584768 | bytes 10486784 | tf_op jit(solution)/shard_map/dot_general | solution.py:39
  443.8 0.0 copy-start.12
  443.8 0.4 slice.74
  444.2 0.9 copy-done.12
  445.1 0.2 slice_select_fusion
  445.3 2.3 pad_maximum_fusion
  447.6 34.0 %reduce-scatter.2.cloned.1.call-done = f32[4,32,1024]{2,1,0:T(8,128)} async-done(((f32[4,256,1024]{2,1,0:T(8,128)}), f32[4,32,1024]{2,1,0:T(8,128)}) %reduce-scatter.2.cloned.1.call-update) | async-done | bytes 524304 | tf_op jit(solution)/shard_map/reduce_scatter | solution.py:57
  (27 shorter events, 0.1 us)
Async XLA Ops:
  7.2 87.0 %all-gather.9.cloned.1.call-start = ((), (), s32[]{:S(2)}) async-start(), calls=%async_computation.2 | async-start | bytes 5242880 | tf_op jit(solution)/shard_map/all_gather | solution.py:9
  10.6 180.2 %all-gather.11.cloned.1.call-start = ((), (), s32[]{:S(2)}) async-start(), calls=%async_computation.3 | async-start | bytes 5242880 | tf_op jit(solution)/shard_map/all_gather | solution.py:9
  96.9 7.6 %copy-start.4 = (f32[256,1024]{1,0:T(8,128)}, f32[256,1024]{1,0:T(8,128)S(1)}, u32[]{:S(2)}) copy-start(f32[256,1024]{1,0:T(8,128)S(1)} %reduce_sum.36) | copy-start | bytes 3145732
  104.6 1.9 copy-start.3
  106.6 1.0 copy-start.11
  111.4 188.7 %all-gather.13.cloned.1.call-start = ((), (), s32[]{:S(2)}) async-start(), calls=%async_computation.4 | async-start | bytes 5242880 | tf_op jit(solution)/shard_map/all_gather | solution.py:9
  196.5 8.4 %slice-start.2 = ((f32[1024,1024]{1,0:T(8,128)}), f32[768,1024]{1,0:T(8,128)S(1)}, s32[]{:S(2)}) async-start(f32[1024,1024]{1,0:T(8,128)} %copy-done.3), calls=%async_computation.8 | async-start | bytes 6291456 | tf_op jit(solution)/shard_map/slice | solution.py:48
  204.9 10.9 %copy-start.13 = (f32[256,1024]{1,0:T(8,128)S(1)}, f32[256,1024]{1,0:T(8,128)}, u32[]{:S(2)}) copy-start(f32[256,1024]{1,0:T(8,128)} %copy.6) | copy-start | bytes 3145732
  213.9 1.9 copy-start.2
  216.0 1.0 copy-start.10
  220.7 188.9 %all-gather.15.cloned.1.call-start = ((), (), s32[]{:S(2)}) async-start(), calls=%async_computation.5 | async-start | bytes 5242880 | tf_op jit(solution)/shard_map/all_gather | solution.py:9
  306.1 8.4 %slice-start.1 = ((f32[1024,1024]{1,0:T(8,128)}), f32[768,1024]{1,0:T(8,128)S(1)}, s32[]{:S(2)}) async-start(f32[1024,1024]{1,0:T(8,128)} %copy-done.2), calls=%async_computation.7 | async-start | bytes 6291456 | tf_op jit(solution)/shard_map/slice | solution.py:48
  314.5 10.9 %copy-start.14 = (f32[256,1024]{1,0:T(8,128)S(1)}, f32[256,1024]{1,0:T(8,128)}, u32[]{:S(2)}) copy-start(f32[256,1024]{1,0:T(8,128)} %copy.7) | copy-start | bytes 3145732
  323.4 1.9 copy-start.1
  325.4 5.0 %copy-start.5 = (f32[256,1024]{1,0:T(8,128)S(1)}, f32[256,1024]{1,0:T(8,128)}, u32[]{:S(2)}) copy-start(f32[256,1024]{1,0:T(8,128)} %copy-done.4) | copy-start | bytes 3145732
  325.5 1.0 copy-start.9
  330.2 6.4 %copy-start.6 = (f32[256,1024]{0,1:T(8,128)S(1)}, f32[256,1024]{0,1:T(8,128)}, u32[]{:S(2)}) copy-start(f32[256,1024]{0,1:T(8,128)} %reduce_sum.37) | copy-start | bytes 3145732
  330.3 151.4 %reduce-scatter.2.cloned.1.call-start = ((), (), s32[]{:S(2)}) async-start(), calls=%async_computation.1 | async-start | bytes 4718592 | tf_op jit(solution)/shard_map/reduce_scatter | solution.py:57
  330.3 6.3 %copy-start = (f32[1024,1024]{1,0:T(8,128)S(1)}, f32[1024,1024]{1,0:T(8,128)}, u32[]{:S(2)}) copy-start(f32[1024,1024]{1,0:T(8,128)} %param.5) | copy-start | bytes 12582916
  336.6 8.1 %copy-start.7 = (f32[256,1024]{0,1:T(8,128)S(1)}, f32[256,1024]{0,1:T(8,128)}, u32[]{:S(2)}) copy-start(f32[256,1024]{0,1:T(8,128)} %reduce_sum.38) | copy-start | bytes 3145732
  419.9 11.8 %copy-start.8 = (f32[256,1024]{0,1:T(8,128)}, f32[256,1024]{0,1:T(8,128)S(1)}, u32[]{:S(2)}) copy-start(f32[256,1024]{0,1:T(8,128)S(1)} %reduce_sum.39) | copy-start | bytes 3145732
  420.0 9.5 %copy-start.15 = (f32[1,256,1024]{2,1,0:T(8,128)S(1)}, f32[1,256,1024]{2,1,0:T(8,128)}, u32[]{:S(2)}) copy-start(f32[1,256,1024]{2,1,0:T(8,128)} %fusion.8) | copy-start | bytes 3145732
  420.0 9.5 %copy-start.16 = (f32[1,256,1024]{2,1,0:T(8,128)S(1)}, f32[1,256,1024]{2,1,0:T(8,128)}, u32[]{:S(2)}) copy-start(f32[1,256,1024]{2,1,0:T(8,128)} %fusion.6) | copy-start | bytes 3145732
  431.8 2.8 slice-start
  443.8 1.3 copy-start.12
Sparse Core Ops, SparseCore 0:
  10.7 83.4 all-gather.8
  111.5 79.2 all-gather.10
  220.8 79.2 all-gather.12
  330.4 79.2 all-gather.14
  431.9 49.6 reduce-scatter.1
